TPU v7x, 32 devices: a whole 2x2x4 slice. The times are simulated.
32 devices in a mesh: batch: 4 (over y, core), proto: 8 (over z, x).
Axes of the slice: x: 2, y: 2, z: 4, core: 2. Of those that a mesh axis runs over, the one named last changes fastest.
Arguments:
- features: bfloat16 [4096, 256], P(('batch', 'proto')), may hold values from -8 to 8
- head_weight: bfloat16 [256, 65536], P('batch', 'proto'), may hold values from -0.375 to 0.375
- student_scores: bfloat16 [2, 4096, 65536], P(None, 'batch', 'proto'), may hold values from -1 to 1
Outputs:
- targets: bfloat16 [4096, 65536], P('batch', 'proto')
- row_loss: float32 [2, 4096], P(None, 'batch')
All inputs are finite; a program needn't handle non-finite values.
Results may differ from a plain program's by a relative error of at most 0.0013.
Values may be sent and summed in bfloat16 or wider, within the bound.
No kernel may reach another device: no remote copies, remote signals or barrier semaphores. Data moves between devices by JAX's collectives and lax.ppermute only.
A program may use at most 192 MiB of HBM per device.

v0:
```python
import jax
import jax.numpy as jnp
from jax import lax
from jax.sharding import PartitionSpec as P

PROTOS = 65536
ITERS = 3
TEACHER_TEMP = 0.07
STUDENT_TEMP = 0.1


def normalize_columns(balance):
    column_sum = lax.psum(jnp.sum(balance, axis=0), "batch")
    return balance / column_sum[None, :]


def crop_totals(balance):
    return lax.psum(jnp.sum(balance, axis=1), "proto")


def local(features, head_weight, student_scores):
    gathered = lax.all_gather(features, "proto", axis=0, tiled=True)
    feat_wide = gathered.astype(jnp.float32)
    fnorm = jnp.sqrt(jnp.sum(feat_wide * feat_wide, axis=1) + 1e-06)
    piece = lax.all_gather(head_weight, "batch", axis=0, tiled=True)
    piece_wide = piece.astype(jnp.float32)
    raw = jnp.dot(gathered, piece, preferred_element_type=jnp.float32)
    squares = jnp.sum(piece_wide * piece_wide, axis=0)
    wnorm = jnp.sqrt(squares + 1e-06)
    balance = jnp.exp(raw / (fnorm[:, None] * wnorm[None, :]) / TEACHER_TEMP)
    logits = student_scores.astype(jnp.float32) / STUDENT_TEMP
    exp_sums = jnp.sum(jnp.exp(logits), axis=2)
    for step in range(ITERS - 1):
        balance = normalize_columns(balance)
        balance = balance / crop_totals(balance)[:, None]
    balance = normalize_columns(balance)
    weighted = jnp.sum(logits * balance[None, :, :], axis=2)
    last_rows, total_exp, total_weighted = lax.psum(
        (jnp.sum(balance, axis=1), exp_sums, weighted), "proto"
    )
    balance = balance / last_rows[:, None]
    row_loss = jnp.log(total_exp) - total_weighted / last_rows[None, :]
    targets = (balance * PROTOS).astype(jnp.bfloat16)
    return (targets, row_loss)


def solution(mesh):
    return jax.shard_map(
        local,
        mesh=mesh,
        in_specs=(P(("batch", "proto"), None), P("batch", "proto"), P(None, "batch", "proto")),
        out_specs=(P("batch", "proto"), P(None, "batch")),
        check_vma=False,
    )
```

profile of v0, /device:TPU:0, one launch (start us, length us, event | category | flops | bytes accessed | tf_op | source)
XLA Modules:
  0.0 311.4 jit_solution(16653263350034114309)
XLA Ops:
  7.2 0.0 all-gather.2.cloned.1.call-start
  7.2 0.7 all-gather.2.cloned.1.call-update
  7.9 33.2 %all_gather.6 = bf16[1024,256]{1,0:T(8,128)(2,1)S(1)} all-gather(bf16[128,256]{1,0:T(8,128)(2,1)} %param.3), channel_id=1, replica_groups=mesh['batch'=4,'proto'=8] {'proto'}, dimensions={0}, use_global_device_ids=true | all-gather | bytes 589824 | tf_op jit(solution)/shard_map/all_gather | solution.py:22
  41.1 0.2 multiply_reduce_fusion.1
  41.4 5.4 %all-gather.2.cloned.1.call-done = bf16[256,8192]{1,0:T(8,128)(2,1)} async-done(((bf16[64,8192]{1,0:T(8,128)(2,1)}), bf16[256,8192]{1,0:T(8,128)(2,1)}) %all-gather.2.cloned.1.call-update) | async-done | bytes 4194320 | tf_op jit(solution)/shard_map/all_gather | solution.py:25
  46.7 3.1 multiply_reduce_fusion
  49.8 17.7 %fusion.16 = (f32[8192]{0:T(1024)S(1)}, f32[1024,8192]{1,0:T(8,128)}) fusion(f32[8192]{0:T(1024)S(1)} %add_sqrt_fusion, f32[1024]{0:T(1024)S(1)} %add_sqrt_fusion.1, bf16[1024,256]{1,0:T(8,128)(2,1)S(1)} %all_gather.6, bf16[256,8192]{1,0:T(8,128)(2,1)} %all-gather.2.cloned.1.call-done), kind=kOutput, calls=%fused_computation.28 | convolution fusion | flops 4328513536 | bytes 38342656 | tf_op jit(solution)/shard_map/dot_general | solution.py:27
  67.5 10.4 %psum.56 = f32[8192]{0:T(1024)S(1)} all-reduce(f32[8192]{0:T(1024)S(1)} %get-tuple-element.9), channel_id=1, replica_groups=mesh['batch'=4,'proto'=8] {'batch'}, use_global_device_ids=true, to_apply=%region_3.0 | all-reduce | flops 8192 | bytes 65536 | tf_op jit(solution)/shard_map/psum | solution.py:13
  77.9 12.2 %divide_reduce_fusion = f32[1024]{0:T(1024)S(1)} fusion(f32[1024,8192]{1,0:T(8,128)} %get-tuple-element.10, f32[8192]{0:T(1024)S(1)} %psum.56), kind=kLoop, calls=%fused_computation.16 | loop fusion | flops 16776192 | bytes 33591296 | tf_op jit(solution)/shard_map/reduce_sum | solution.py:18
  90.1 21.5 %psum.57 = f32[1024]{0:T(1024)S(1)} all-reduce(f32[1024]{0:T(1024)S(1)} %divide_reduce_fusion), channel_id=1, replica_groups=mesh['batch'=4,'proto'=8] {'proto'}, use_global_device_ids=true, to_apply=%region_5.0 | all-reduce | flops 1024 | bytes 8192 | tf_op jit(solution)/shard_map/psum | solution.py:18
  111.6 14.1 %fusion.11 = f32[8192]{0:T(1024)S(1)} fusion(f32[1024,8192]{1,0:T(8,128)} %get-tuple-element.10, f32[1024]{0:T(1024)S(1)} %psum.57, f32[8192]{0:T(1024)S(1)} %psum.56), kind=kLoop, calls=%fused_computation.17 | loop fusion | flops 25157632 | bytes 33624064 | tf_op jit(solution)/shard_map/reduce_sum | solution.py:13
  125.7 10.3 %psum.58 = f32[8192]{0:T(1024)S(1)} all-reduce(f32[8192]{0:T(1024)S(1)} %fusion.11), channel_id=1, replica_groups=mesh['batch'=4,'proto'=8] {'batch'}, use_global_device_ids=true, to_apply=%region_7.0 | all-reduce | flops 8192 | bytes 65536 | tf_op jit(solution)/shard_map/psum | solution.py:13
  136.0 14.1 %fusion.13 = f32[1024]{0:T(1024)S(1)} fusion(f32[1024,8192]{1,0:T(8,128)} %get-tuple-element.10, f32[8192]{0:T(1024)S(1)} %psum.58, f32[1024]{0:T(1024)S(1)} %psum.57, f32[8192]{0:T(1024)S(1)} %psum.56), kind=kLoop, calls=%fused_computation.19 | loop fusion | flops 33553408 | bytes 33628160 | tf_op jit(solution)/shard_map/reduce_sum | solution.py:18
  150.1 17.1 %psum.59 = f32[1024]{0:T(1024)S(1)} all-reduce(f32[1024]{0:T(1024)S(1)} %fusion.13), channel_id=1, replica_groups=mesh['batch'=4,'proto'=8] {'proto'}, use_global_device_ids=true, to_apply=%region_9.0 | all-reduce | flops 1024 | bytes 8192 | tf_op jit(solution)/shard_map/psum | solution.py:18
  167.3 14.5 %fusion.14 = f32[8192]{0:T(1024)S(1)} fusion(f32[1024,8192]{1,0:T(8,128)} %get-tuple-element.10, f32[1024]{0:T(1024)S(1)} %psum.59, f32[8192]{0:T(1024)S(1)} %psum.58, f32[1024]{0:T(1024)S(1)} %psum.57, f32[8192]{0:T(1024)S(1)} %psum.56), kind=kLoop, calls=%fused_computation.20 | loop fusion | flops 41934848 | bytes 33660928 | tf_op jit(solution)/shard_map/reduce_sum | solution.py:13
  181.7 10.4 %psum.60 = f32[8192]{0:T(1024)S(1)} all-reduce(f32[8192]{0:T(1024)S(1)} %fusion.14), channel_id=1, replica_groups=mesh['batch'=4,'proto'=8] {'batch'}, use_global_device_ids=true, to_apply=%region_11.0 | all-reduce | flops 8192 | bytes 65536 | tf_op jit(solution)/shard_map/psum | solution.py:13
  192.2 28.0 %broadcast_multiply_fusion = (f32[1024,8192]{1,0:T(8,128)}, f32[1024]{0:T(1024)S(1)}) fusion(f32[1024,8192]{1,0:T(8,128)} %get-tuple-element.10, f32[8192]{0:T(1024)S(1)} %psum.60, f32[1024]{0:T(1024)S(1)} %psum.59, f32[8192]{0:T(1024)S(1)} %psum.58, f32[1024]{0:T(1024)S(1)} %psum.57, f32[8192]{0:T(1024)S(1)} %psum.56), kind=kLoop, calls=%fused_computation.21 | loop fusion | flops 58719232 | bytes 67219456 | tf_op jit(solution)/shard_map/mul | solution.py:37
  220.2 27.8 %fusion.1 = (f32[2,1024]{1,0:T(2,128)S(1)}, f32[2,1024]{1,0:T(2,128)S(1)}) fusion(bf16[2,1024,8192]{2,1,0:T(8,128)(2,1)} %param.5, f32[1024,8192]{1,0:T(8,128)} %get-tuple-element.7), kind=kLoop, calls=%fused_computation.3 | loop fusion | flops 83881984 | bytes 67125248 | tf_op jit(solution)/shard_map/reduce_sum | solution.py:32
  248.0 34.9 %all-reduce = (f32[1024]{0:T(1024)S(1)}, f32[2,1024]{1,0:T(2,128)S(1)}, f32[2,1024]{1,0:T(2,128)S(1)}) all-reduce(f32[1024]{0:T(1024)S(1)} %get-tuple-element.8, f32[2,1024]{1,0:T(2,128)S(1)} %get-tuple-element.3, f32[2,1024]{1,0:T(2,128)S(1)} %get-tuple-element.2), channel_id=1, replica_groups=mesh['batch'=4,'proto'=8] {'proto'}, use_global_device_ids=true, to_apply=%region_13.0 | all-reduce | flops 5120 | bytes 40960 | tf_op jit(solution)/shard_map/psum | solution.py:38
  282.9 21.1 %fusion.12 = bf16[1024,8192]{1,0:T(8,128)(2,1)} fusion(f32[1024,8192]{1,0:T(8,128)} %get-tuple-element.10, f32[1024]{0:T(1024)S(1)} %get-tuple-element.4, f32[8192]{0:T(1024)S(1)} %psum.60, f32[1024]{0:T(1024)S(1)} %psum.59, f32[8192]{0:T(1024)S(1)} %psum.58, f32[1024]{0:T(1024)S(1)} %psum.57, f32[8192]{0:T(1024)S(1)} %psum.56), kind=kLoop, calls=%fused_computation.18 | loop fusion | flops 67108864 | bytes 50442240 | tf_op jit(solution)/shard_map/convert_element_type | solution.py:43
  303.9 0.6 divide_subtract_fusion
  (2 shorter events, 0.0 us)
Async XLA Ops:
  7.2 39.6 %all-gather.2.cloned.1.call-start = ((), (), s32[]{:S(2)}) async-start(), calls=%async_computation | async-start | bytes 5242880 | tf_op jit(solution)/shard_map/all_gather | solution.py:25
Sparse Core Ops, SparseCore 0:
  9.5 37.1 all-gather.1
where the time goes:
time: 312 us; the launch traced here: 311 us
  blocking collectives  138 us (44%)
  other arithmetic  136 us (44%)
  matrix products  17.7 us (6%)
  between operations  14.1 us (5%)
  waiting for transfers between devices  6.05 us (2%)
    psum x2, blocking collectives, crop_totals(): return lax.psum(jnp.sum(balance, axis=1), 'proto')  38.7 us
    psum x1, blocking collectives, local(): lax.psum((jnp.sum(balance, axis=1), exp_sums, weighted), 'proto')  34.9 us
    all_gather x1, blocking collectives, local(): gathered = lax.all_gather(features, 'proto', axis=0, tiled=True)  33.2 us
    psum x3, blocking collectives, normalize_columns(): column_sum = lax.psum(jnp.sum(balance, axis=0), 'batch')  31.1 us
    reduce_sum x2, other arithmetic, normalize_columns(): column_sum = lax.psum(jnp.sum(balance, axis=0), 'batch')  28.5 us
    mul x1, other arithmetic, local(): weighted = jnp.sum(logits * balance[None, :, :], axis=2)  28 us
    reduce_sum x1, other arithmetic, local(): exp_sums = jnp.sum(jnp.exp(logits), axis=2)  27.8 us
    reduce_sum x2, other arithmetic, crop_totals(): return lax.psum(jnp.sum(balance, axis=1), 'proto')  26.3 us
  transfers between devices with their start and end apart: 1, of which 1 were waited for; matrix products, arithmetic and copies ran while one was open for 0% of the time, Pallas kernels for 0%

commit v1 on v0

--- a/solution.py
+++ b/solution.py
@@ -15,7 +15,7 @@
 
 
 def crop_totals(balance):
-    return lax.psum(jnp.sum(balance, axis=1), "proto")
+    return jnp.sum(lax.all_gather(jnp.sum(balance, axis=1), "proto"), axis=0)
 
 
 def local(features, head_weight, student_scores):

time: 312 us -> 337 us (1.080)
  blocking collectives: 138 us -> 163 us
    all_gather x0 -> x2, blocking collectives: none -> 61.4 us  [crop_totals(): return jnp.sum(lax.all_gather(jnp.sum(balance, axis=1), 'proto'), axis=0)]
    psum x2 -> x0, blocking collectives: 38.7 us -> none  [crop_totals(): return lax.psum(jnp.sum(balance, axis=1), 'proto')]
    reduce_sum x2 -> x4, other arithmetic: 26.3 us -> 26.4 us  [crop_totals(): return jnp.sum(lax.all_gather(jnp.sum(balance, axis=1), 'proto'), axis=0)]
where the time goes in v1:
time: 337 us; the launch traced here: 336 us
  blocking collectives  163 us (48%)
  other arithmetic  136 us (40%)
  matrix products  17.7 us (5%)
  between operations  14.1 us (4%)
  waiting for transfers between devices  6.05 us (2%)
    all_gather x2, blocking collectives, crop_totals(): return jnp.sum(lax.all_gather(jnp.sum(balance, axis=1), 'proto'), axis=0)  61.4 us
    psum x1, blocking collectives, local(): lax.psum((jnp.sum(balance, axis=1), exp_sums, weighted), 'proto')  37 us
    all_gather x1, blocking collectives, local(): gathered = lax.all_gather(features, 'proto', axis=0, tiled=True)  33.2 us
    psum x3, blocking collectives, normalize_columns(): column_sum = lax.psum(jnp.sum(balance, axis=0), 'batch')  31.1 us
    reduce_sum x2, other arithmetic, normalize_columns(): column_sum = lax.psum(jnp.sum(balance, axis=0), 'batch')  28.5 us
    mul x1, other arithmetic, local(): weighted = jnp.sum(logits * balance[None, :, :], axis=2)  28 us
    reduce_sum x1, other arithmetic, local(): exp_sums = jnp.sum(jnp.exp(logits), axis=2)  27.8 us
    reduce_sum x4, other arithmetic, crop_totals(): return jnp.sum(lax.all_gather(jnp.sum(balance, axis=1), 'proto'), axis=0)  26.4 us
  transfers between devices with their start and end apart: 1, of which 1 were waited for; matrix products, arithmetic and copies ran while one was open for 0% of the time, Pallas kernels for 0%

profile of v1, /device:TPU:0, one launch (start us, length us, event | category | flops | bytes accessed | tf_op | source)
XLA Modules:
  0.0 336.4 jit_solution(13763494038128599305)
XLA Ops:
  7.2 0.0 all-gather.4.cloned.1.call-start
  7.2 0.7 all-gather.4.cloned.1.call-update
  7.9 33.2 %all_gather.18 = bf16[1024,256]{1,0:T(8,128)(2,1)S(1)} all-gather(bf16[128,256]{1,0:T(8,128)(2,1)} %param.3), channel_id=1, replica_groups=mesh['batch'=4,'proto'=8] {'proto'}, dimensions={0}, use_global_device_ids=true | all-gather | bytes 589824 | tf_op jit(solution)/shard_map/all_gather | solution.py:22
  41.1 0.2 multiply_reduce_fusion.1
  41.4 5.4 %all-gather.4.cloned.1.call-done = bf16[256,8192]{1,0:T(8,128)(2,1)} async-done(((bf16[64,8192]{1,0:T(8,128)(2,1)}), bf16[256,8192]{1,0:T(8,128)(2,1)}) %all-gather.4.cloned.1.call-update) | async-done | bytes 4194320 | tf_op jit(solution)/shard_map/all_gather | solution.py:25
  46.7 3.1 multiply_reduce_fusion
  49.8 17.7 %fusion.16 = (f32[8192]{0:T(1024)S(1)}, f32[1024,8192]{1,0:T(8,128)}) fusion(f32[8192]{0:T(1024)S(1)} %add_sqrt_fusion, f32[1024]{0:T(1024)S(1)} %add_sqrt_fusion.1, bf16[1024,256]{1,0:T(8,128)(2,1)S(1)} %all_gather.18, bf16[256,8192]{1,0:T(8,128)(2,1)} %all-gather.4.cloned.1.call-done), kind=kOutput, calls=%fused_computation.28 | convolution fusion | flops 4328513536 | bytes 38342656 | tf_op jit(solution)/shard_map/dot_general | solution.py:27
  67.5 10.4 %psum.42 = f32[8192]{0:T(1024)S(1)} all-reduce(f32[8192]{0:T(1024)S(1)} %get-tuple-element.9), channel_id=1, replica_groups=mesh['batch'=4,'proto'=8] {'batch'}, use_global_device_ids=true, to_apply=%region_3.0 | all-reduce | flops 8192 | bytes 65536 | tf_op jit(solution)/shard_map/psum | solution.py:13
  77.9 12.2 %divide_reduce_fusion = f32[1024]{0:T(1024)S(1)} fusion(f32[1024,8192]{1,0:T(8,128)} %get-tuple-element.10, f32[8192]{0:T(1024)S(1)} %psum.42), kind=kLoop, calls=%fused_computation.16 | loop fusion | flops 16776192 | bytes 33591296 | tf_op jit(solution)/shard_map/reduce_sum | solution.py:18
  90.1 30.8 %all-gather = f32[8192]{0:T(1024)S(1)} all-gather(f32[1024]{0:T(1024)S(1)} %divide_reduce_fusion), channel_id=2, replica_groups=mesh['batch'=4,'proto'=8] {'proto'}, dimensions={0}, use_global_device_ids=true | all-gather | bytes 36864 | tf_op jit(solution)/shard_map/all_gather | solution.py:18
  121.0 14.1 %fusion.11 = f32[8192]{0:T(1024)S(1)} fusion(f32[1024,8192]{1,0:T(8,128)} %get-tuple-element.10, f32[1024]{0:T(1024)S(1)} %reduce_sum.112, f32[8192]{0:T(1024)S(1)} %psum.42), kind=kLoop, calls=%fused_computation.17 | loop fusion | flops 25157632 | bytes 33624064 | tf_op jit(solution)/shard_map/reduce_sum | solution.py:13
  135.1 10.3 %psum.43 = f32[8192]{0:T(1024)S(1)} all-reduce(f32[8192]{0:T(1024)S(1)} %fusion.11), channel_id=1, replica_groups=mesh['batch'=4,'proto'=8] {'batch'}, use_global_device_ids=true, to_apply=%region_7.0 | all-reduce | flops 8192 | bytes 65536 | tf_op jit(solution)/shard_map/psum | solution.py:13
  145.3 14.1 %fusion.13 = f32[1024]{0:T(1024)S(1)} fusion(f32[1024,8192]{1,0:T(8,128)} %get-tuple-element.10, f32[8192]{0:T(1024)S(1)} %psum.43, f32[1024]{0:T(1024)S(1)} %reduce_sum.112, f32[8192]{0:T(1024)S(1)} %psum.42), kind=kLoop, calls=%fused_computation.19 | loop fusion | flops 33553408 | bytes 33628160 | tf_op jit(solution)/shard_map/reduce_sum | solution.py:18
  159.5 30.6 %all-gather.1 = f32[8192]{0:T(1024)S(1)} all-gather(f32[1024]{0:T(1024)S(1)} %fusion.13), channel_id=3, replica_groups=mesh['batch'=4,'proto'=8] {'proto'}, dimensions={0}, use_global_device_ids=true | all-gather | bytes 36864 | tf_op jit(solution)/shard_map/all_gather | solution.py:18
  190.1 14.5 %fusion.14 = f32[8192]{0:T(1024)S(1)} fusion(f32[1024,8192]{1,0:T(8,128)} %get-tuple-element.10, f32[1024]{0:T(1024)S(1)} %reduce_sum.115, f32[8192]{0:T(1024)S(1)} %psum.43, f32[1024]{0:T(1024)S(1)} %reduce_sum.112, f32[8192]{0:T(1024)S(1)} %psum.42), kind=kLoop, calls=%fused_computation.20 | loop fusion | flops 41934848 | bytes 33660928 | tf_op jit(solution)/shard_map/reduce_sum | solution.py:13
  204.6 10.4 %psum.44 = f32[8192]{0:T(1024)S(1)} all-reduce(f32[8192]{0:T(1024)S(1)} %fusion.14), channel_id=1, replica_groups=mesh['batch'=4,'proto'=8] {'batch'}, use_global_device_ids=true, to_apply=%region_11.0 | all-reduce | flops 8192 | bytes 65536 | tf_op jit(solution)/shard_map/psum | solution.py:13
  215.1 28.0 %broadcast_multiply_fusion = (f32[1024,8192]{1,0:T(8,128)}, f32[1024]{0:T(1024)S(1)}) fusion(f32[1024,8192]{1,0:T(8,128)} %get-tuple-element.10, f32[8192]{0:T(1024)S(1)} %psum.44, f32[1024]{0:T(1024)S(1)} %reduce_sum.115, f32[8192]{0:T(1024)S(1)} %psum.43, f32[1024]{0:T(1024)S(1)} %reduce_sum.112, f32[8192]{0:T(1024)S(1)} %psum.42), kind=kLoop, calls=%fused_computation.21 | loop fusion | flops 58719232 | bytes 67219456 | tf_op jit(solution)/shard_map/mul | solution.py:37
  243.1 27.8 %fusion.1 = (f32[2,1024]{1,0:T(2,128)S(1)}, f32[2,1024]{1,0:T(2,128)S(1)}) fusion(bf16[2,1024,8192]{2,1,0:T(8,128)(2,1)} %param.5, f32[1024,8192]{1,0:T(8,128)} %get-tuple-element.7), kind=kLoop, calls=%fused_computation.3 | loop fusion | flops 83881984 | bytes 67125248 | tf_op jit(solution)/shard_map/reduce_sum | solution.py:32
  270.9 37.0 %all-reduce = (f32[1024]{0:T(1024)S(1)}, f32[2,1024]{1,0:T(2,128)S(1)}, f32[2,1024]{1,0:T(2,128)S(1)}) all-reduce(f32[1024]{0:T(1024)S(1)} %get-tuple-element.8, f32[2,1024]{1,0:T(2,128)S(1)} %get-tuple-element.3, f32[2,1024]{1,0:T(2,128)S(1)} %get-tuple-element.2), channel_id=1, replica_groups=mesh['batch'=4,'proto'=8] {'proto'}, use_global_device_ids=true, to_apply=%region_13.0 | all-reduce | flops 5120 | bytes 40960 | tf_op jit(solution)/shard_map/psum | solution.py:38
  307.9 21.1 %fusion.12 = bf16[1024,8192]{1,0:T(8,128)(2,1)} fusion(f32[1024,8192]{1,0:T(8,128)} %get-tuple-element.10, f32[1024]{0:T(1024)S(1)} %get-tuple-element.4, f32[8192]{0:T(1024)S(1)} %psum.44, f32[1024]{0:T(1024)S(1)} %reduce_sum.115, f32[8192]{0:T(1024)S(1)} %psum.43, f32[1024]{0:T(1024)S(1)} %reduce_sum.112, f32[8192]{0:T(1024)S(1)} %psum.42), kind=kLoop, calls=%fused_computation.18 | loop fusion | flops 67108864 | bytes 50442240 | tf_op jit(solution)/shard_map/convert_element_type | solution.py:43
  329.0 0.6 divide_subtract_fusion
  (6 shorter events, 0.1 us)
Async XLA Ops:
  7.2 39.6 %all-gather.4.cloned.1.call-start = ((), (), s32[]{:S(2)}) async-start(), calls=%async_computation | async-start | bytes 5242880 | tf_op jit(solution)/shard_map/all_gather | solution.py:25
Sparse Core Ops, SparseCore 0:
  9.5 37.1 all-gather.3
